TPU v7x, 32 devices: a whole 2x2x4 slice. The times are simulated.
32 devices in a mesh: groups: 2 (over y), dp: 8 (over z, x), section: 2 (over core).
Axes of the slice: x: 2, y: 2, z: 4, core: 2. Of those that a mesh axis runs over, the one named last changes fastest.
Arguments:
- latents: bfloat16 [2048, 3072], P(('groups', 'dp')), parts along dimension 0, may hold values from -6 to 6
- out_grad: float32 [2048, 3072], P(('groups', 'dp')), parts along dimension 0, may hold values from -0.3 to 0.3
- frozen_weight: bfloat16 [2, 3072, 1536], P('section', 'dp'), may hold values from -0.109375 to 0.109375
- norm_gain: float32 [2, 3072], P('section'), may hold values from 0.5 to 1.5
- time_gate: float32 [2, 50], P('section'), may hold values from 0.5 to 2
- down_factors: bfloat16 [2, 96, 64, 3072], P('section', ('groups', 'dp')), parts along dimension 1, may hold values from -0.109375 to 0.109375
- up_factors: bfloat16 [2, 96, 64, 1536], P('section', ('groups', 'dp')), parts along dimension 1, may hold values from -0.75 to 0.75
- block_jobs: int32 [16], P('groups'), parts along dimension 0, may hold values from 0 to 47
- owners: int32 [96], P('groups'), parts along dimension 0, may hold values from 0 to 47, as said below
- block_steps: int32 [16], P(('groups', 'dp')), parts along dimension 0, may hold values from 0 to 49
- block_fill: int32 [16], P(('groups', 'dp')), parts along dimension 0, may hold values from 1 to 128, as said below
Outputs:
- grad_down: float32 [2, 96, 64, 3072], P('section', ('groups', 'dp')), parts along dimension 1
- grad_up: float32 [2, 96, 64, 1536], P('section', ('groups', 'dp')), parts along dimension 1
There are 2 independent parts, one for each index of `groups`. A program takes and returns all parts, laid end to end along the dimension named above; an argument that names none is the same for every part. Nothing has to cross between parts.
Inputs may be any that keep to these rules, and one draw needn't show every extreme that they name: `owners`: no two adapters share a slot; slot 0 and the last slot always hold one. `block_fill`: the live rows come first in their block; in every draw some block is full and some holds a single live row.
All inputs are finite; a program needn't handle non-finite values.
Results may differ from a plain program's by a relative error of at most 0.006.
Values may be sent and summed in bfloat16 or wider, within the bound.
No kernel may reach another device: no remote copies, remote signals or barrier semaphores. Data moves between devices by JAX's collectives and lax.ppermute only.
A program may use at most 128 MiB of HBM per device.

v0:
```python
import jax
import jax.numpy as jnp
from jax import lax
from jax.sharding import PartitionSpec as P

epsilon = 1e-06


def passed_along(value, axis, steps):
    count = lax.axis_size(axis)
    leading, last = (max(0, -steps), min(count, count - steps))
    return lax.ppermute(value, axis, [(source, source + steps) for source in range(leading, last)])


def matrix_product(spec, left_op, right_op):
    return jnp.einsum(spec, left_op, right_op, preferred_element_type=jnp.float32)


def forward_pass(inputs, frozen_layer, gain_row, down_projection_block, up_block, scales):
    out_width = up_block.shape[2]
    block_total, row_count, model_width = inputs.shape
    values = inputs.astype(jnp.float32)
    inverse = lax.rsqrt(jnp.mean(values * values, axis=2) + epsilon)
    normalized_input = (values * inverse[:, :, None] * gain_row).astype(jnp.bfloat16)
    frozen_out = jnp.dot(
        normalized_input.reshape(block_total * row_count, model_width),
        frozen_layer,
        preferred_element_type=jnp.float32,
    )
    frozen_out = frozen_out.reshape(block_total, row_count, out_width)
    reduced_features = matrix_product(
        "uyi,uoi->uyo", normalized_input, down_projection_block
    ).astype(jnp.bfloat16)
    extra = matrix_product("bmq,bqh->bmh", reduced_features, up_block)
    update = scales[:, None, None] * (frozen_out + extra)
    window_out = (values[:, :, :out_width] + update).astype(jnp.bfloat16)
    outputs = jnp.concatenate([window_out, inputs[:, :, out_width:]], axis=2)
    return (outputs, (inputs, normalized_input, inverse, reduced_features))


def backward_pass(
    stored, cotangent, frozen_layer, gain_row, down_projection_block, up_block, scales
):
    inputs, normalized_input, inverse, reduced_features = stored
    out_width = up_block.shape[2]
    block_total, row_count, model_width = inputs.shape
    values = inputs.astype(jnp.float32)
    delta_output = (scales[:, None, None] * cotangent[:, :, :out_width]).astype(jnp.bfloat16)
    grad_upper = matrix_product("bmq,bmh->bqh", reduced_features, delta_output)
    low_rank_delta = matrix_product("bmh,bqh->bmq", delta_output, up_block).astype(jnp.bfloat16)
    lower_gradient = matrix_product("hoc,hou->hcu", low_rank_delta, normalized_input)
    through = lax.dot_general(
        delta_output.reshape(block_total * row_count, out_width),
        frozen_layer,
        (((1,), (1,)), ((), ())),
        preferred_element_type=jnp.float32,
    )
    delta_normalized = through.reshape(block_total, row_count, model_width) + matrix_product(
        "rha,rak->rhk", low_rank_delta, down_projection_block
    )
    scaled = gain_row * delta_normalized
    inner = jnp.mean(values * scaled, axis=2)
    cubed = inverse * inverse * inverse
    delta_in = inverse[:, :, None] * scaled - values * (cubed * inner)[:, :, None]
    carried = (cotangent + delta_in).astype(jnp.bfloat16)
    return (carried, lower_gradient, grad_upper)


def body(
    latents,
    out_grad,
    frozen_weight,
    norm_gain,
    time_gate,
    down_factors,
    up_factors,
    block_jobs,
    owners,
    block_steps,
    block_fill,
):
    position = lax.axis_index("section")
    lane_count = lax.axis_size("dp")
    slot_local = down_factors.shape[1]
    low_rank = down_factors.shape[2]
    model_width = down_factors.shape[3]
    blocks_dev = block_fill.shape[0]
    block_rows = latents.shape[0] // blocks_dev
    is_first = position == 0
    frozen_layer = lax.all_gather(frozen_weight[0], "dp", axis=0, tiled=True)
    gain_row = norm_gain[0]
    gate_row = time_gate[0]
    chosen = block_steps[:, None] == jnp.arange(gate_row.shape[0], dtype=jnp.int32)[None, :]
    scales = jnp.sum(jnp.where(chosen, gate_row[None, :], 0.0), axis=1)
    matches = block_jobs[:, None] == jnp.arange(owners.shape[0], dtype=jnp.int32)[None, :]
    slot_of = jnp.sum(jnp.where(matches, owners[None, :], 0), axis=1)
    spread_down, spread_up = (
        lax.all_to_all(down_factors[0], "dp", split_axis=2, concat_axis=0, tiled=True),
        lax.all_to_all(up_factors[0], "dp", split_axis=2, concat_axis=0, tiled=True),
    )
    down_projection_block, up_block = (
        lax.all_to_all(spread_down[slot_of], "dp", split_axis=0, concat_axis=2, tiled=True),
        lax.all_to_all(spread_up[slot_of], "dp", split_axis=0, concat_axis=2, tiled=True),
    )
    micro_count = 1
    micro_rows = block_rows // micro_count
    block_view = latents.reshape(blocks_dev, block_rows, model_width)
    live_rows = jnp.arange(block_rows, dtype=jnp.int32)[None, :] < block_fill[:, None]
    masked = jnp.where(
        live_rows[:, :, None], out_grad.reshape(blocks_dev, block_rows, model_width), 0.0
    )
    incoming = jnp.zeros((blocks_dev, micro_rows, model_width), jnp.bfloat16)
    kept = []
    for turn_index in range(micro_count + 1):
        source = jnp.where(is_first, block_view, incoming)
        outputs, stored = forward_pass(
            source, frozen_layer, gain_row, down_projection_block, up_block, scales
        )
        kept.append(stored)
        if turn_index < micro_count:
            incoming = passed_along(outputs, "section", 1)
    states = [
        jax.tree.map(lambda former, latter: jnp.where(is_first, former, latter), kept[0], kept[1])
    ]
    returned = jnp.zeros((blocks_dev, micro_rows, model_width), jnp.bfloat16)
    sum_down = jnp.zeros((blocks_dev, low_rank, model_width), jnp.float32)
    sum_up = jnp.zeros((blocks_dev, low_rank, up_block.shape[2]), jnp.float32)
    for turn_index in range(micro_count + 1):
        late_micro = min(turn_index, micro_count - 1)
        early_micro = max(turn_index - 1, 0)
        current = jax.tree.map(
            lambda former, latter: jnp.where(is_first, former, latter),
            states[early_micro],
            states[late_micro],
        )
        cotangent = jnp.where(is_first, returned.astype(jnp.float32), masked)
        carried, lower_gradient, grad_upper = backward_pass(
            current, cotangent, frozen_layer, gain_row, down_projection_block, up_block, scales
        )
        useful = jnp.where(is_first, turn_index >= 1, turn_index < micro_count)
        sum_down = sum_down + jnp.where(useful, lower_gradient, 0.0)
        sum_up = sum_up + jnp.where(useful, grad_upper, 0.0)
        if turn_index < micro_count:
            returned = passed_along(carried, "section", -1)
    pieces_down, pieces_up = (
        lax.all_to_all(sum_down, "dp", split_axis=2, concat_axis=0, tiled=True),
        lax.all_to_all(sum_up, "dp", split_axis=2, concat_axis=0, tiled=True),
    )
    slot_total = lane_count * slot_local
    onehot = (jnp.arange(slot_total, dtype=jnp.int32)[:, None] == slot_of[None, :]).astype(
        jnp.float32
    )
    block_total = pieces_down.shape[0]
    slot_down = jnp.dot(
        onehot,
        pieces_down.reshape(block_total, -1),
        precision=lax.Precision.HIGHEST,
        preferred_element_type=jnp.float32,
    )
    slot_up = jnp.dot(
        onehot,
        pieces_up.reshape(block_total, -1),
        precision=lax.Precision.HIGHEST,
        preferred_element_type=jnp.float32,
    )
    slot_down = slot_down.reshape(slot_total, low_rank, pieces_down.shape[2])
    slot_up = slot_up.reshape(slot_total, low_rank, pieces_up.shape[2])
    owned_down, owned_up = (
        lax.all_to_all(slot_down, "dp", split_axis=0, concat_axis=2, tiled=True),
        lax.all_to_all(slot_up, "dp", split_axis=0, concat_axis=2, tiled=True),
    )
    return (owned_down[None], owned_up[None])


def solution(mesh):
    placed = (
        P(("groups", "dp"), None),
        P(("groups", "dp"), None),
        P("section", "dp", None),
        P("section", None),
        P("section", None),
        P("section", ("groups", "dp"), None, None),
        P("section", ("groups", "dp"), None, None),
        P("groups"),
        P("groups"),
        P(("groups", "dp")),
        P(("groups", "dp")),
    )
    return jax.shard_map(
        body,
        mesh=mesh,
        in_specs=placed,
        out_specs=(
            P("section", ("groups", "dp"), None, None),
            P("section", ("groups", "dp"), None, None),
        ),
        check_vma=False,
    )
```

profile of v0, /device:TPU:0, one launch (start us, length us, event | category | flops | bytes accessed | tf_op | source)
XLA Modules:
  0.0 537.3 jit_solution(2931471331591064361)
XLA Ops:
  8.4 3.4 copy.64
  11.9 2.0 bitcast_bitcast_fusion.1
  13.9 3.1 reshape.236
  17.0 7.5 %all-to-all-start = ((bf16[8,2,36864]{2,1,0:T(2,128)(2,1)}), bf16[8,2,36864]{2,1,0:T(2,128)(2,1)S(1)}, u32[]{:S(2)}, u32[]{:S(2)}) async-start(bf16[8,2,36864]{2,1,0:T(2,128)(2,1)} %reshape.236), calls=%async_computation | async-start | bytes 2359296 | tf_op jit(solution)/shard_map/all_to_all | solution.py:99
  24.5 6.0 %copy.68 = bf16[1,6,64,3072]{2,1,3,0:T(8,128)(2,1)} copy(bf16[1,6,64,3072]{3,2,1,0:T(8,128)(2,1)S(1)} %copy-done.7) | data formatting | bytes 4718592 | tf_op args[5]
  30.5 6.4 %bitcast_bitcast_fusion = bf16[3072,6,64]{2,1,0:T(8,128)(2,1)} fusion(bf16[1,6,64,3072]{2,1,3,0:T(8,128)(2,1)} %copy.68), kind=kLoop, calls=%fused_computation.81 | loop fusion | bytes 4718592
  37.0 8.5 %reshape.238 = bf16[8,2,73728]{2,1,0:T(2,128)(2,1)} reshape(bf16[3072,6,64]{2,1,0:T(8,128)(2,1)} %bitcast_bitcast_fusion) | data formatting | bytes 4718592
  45.5 38.7 %all-to-all-done = bf16[8,2,36864]{2,1,0:T(2,128)(2,1)S(1)} async-done(((bf16[8,2,36864]{2,1,0:T(2,128)(2,1)}), bf16[8,2,36864]{2,1,0:T(2,128)(2,1)S(1)}, u32[]{:S(2)}, u32[]{:S(2)}) %all-to-all-start) | async-done | bytes 1179680 | tf_op jit(solution)/shard_map/all_to_all | solution.py:99
  84.2 1.0 copy-done.3
  85.2 4.4 all-to-all-start.2
  91.0 2.1 select_bitcast_fusion
  93.1 3.6 reshape.237
  96.6 2.7 copy.66
  99.3 2.7 gather_fusion
  102.1 98.8 %all-to-all-done.2 = bf16[8,2,73728]{2,1,0:T(2,128)(2,1)} async-done(((bf16[8,2,73728]{2,1,0:T(2,128)(2,1)}), bf16[8,2,73728]{2,1,0:T(2,128)(2,1)}, u32[]{:S(2)}, u32[]{:S(2)}) %all-to-all-start.2) | async-done | bytes 2359328 | tf_op jit(solution)/shard_map/all_to_all | solution.py:98
  200.9 9.0 %all-to-all-start.1 = ((bf16[8,64,192]{2,1,0:T(8,128)(2,1)}), bf16[8,64,192]{2,1,0:T(8,128)(2,1)S(1)}, u32[]{:S(2)}, u32[]{:S(2)}) async-start(bf16[8,64,192]{2,1,0:T(8,128)(2,1)} %gather_fusion), calls=%async_computation.1 | async-start | bytes 524288 | tf_op jit(solution)/shard_map/all_to_all | solution.py:103
  210.0 1.3 convert_bitcast_fusion
  212.0 0.8 slice.22
  213.6 8.2 %reshape.239 = bf16[3072,6,64]{2,1,0:T(8,128)(2,1)} reshape(bf16[8,2,73728]{2,1,0:T(2,128)(2,1)} %all-to-all-done.2) | data formatting | bytes 4718592
  221.9 6.7 %copy.70 = bf16[8,6,64,384]{3,2,1,0:T(8,128)(2,1)} copy(bf16[8,6,64,384]{2,1,3,0:T(8,128)(2,1)} %bitcast.151) | data formatting | bytes 4718592 | tf_op jit(solution)/shard_map/all_to_all | solution.py:98
  228.5 3.1 gather_fusion.1
  231.7 6.0 %all-to-all-start.3 = ((bf16[8,64,384]{2,1,0:T(8,128)(2,1)}), bf16[8,64,384]{2,1,0:T(8,128)(2,1)S(1)}, u32[]{:S(2)}, u32[]{:S(2)}) async-start(bf16[8,64,384]{2,1,0:T(8,128)(2,1)} %gather_fusion.1), calls=%async_computation.3 | async-start | bytes 786432 | tf_op jit(solution)/shard_map/all_to_all | solution.py:102
  238.3 1.8 copy.67
  240.1 1.2 reshape.210
  241.3 7.4 %all-to-all-done.3 = bf16[8,64,384]{2,1,0:T(8,128)(2,1)S(1)} async-done(((bf16[8,64,384]{2,1,0:T(8,128)(2,1)}), bf16[8,64,384]{2,1,0:T(8,128)(2,1)S(1)}, u32[]{:S(2)}, u32[]{:S(2)}) %all-to-all-start.3) | async-done | bytes 393248 | tf_op jit(solution)/shard_map/all_to_all | solution.py:102
  248.8 0.7 copy-done.11
  250.1 5.3 fusion.2
  255.4 1.4 fusion.10
  257.0 1.3 collective-permute-start
  258.7 3.1 fusion
  261.8 0.8 fusion.16
  263.2 1.4 fusion.19
  264.7 1.6 collective-permute-start.1
  266.3 1.5 fusion.23
  267.7 1.6 collective-permute-done.1
  269.3 1.6 fusion.34
  272.9 7.1 %reduce.7 = f32[1536,64]{1,0:T(8,128)S(1)} reduce(f32[1536,1,64]{2,1,0:T(1,128)S(1)} %bitcast.157, f32[]{:T(128)} %broadcast.202), dimensions={1}, to_apply=%bitcast.124.reduce_sub_computation | reduce | bytes 786436
  280.0 1.2 reshape.242
  281.3 4.1 all-to-all-start.6
  285.4 1.7 convolution_select_fusion
  287.1 1.8 fusion.6
  288.9 1.7 copy.72
  290.6 13.6 %reduce.5 = f32[3072,64]{1,0:T(8,128)S(1)} reduce(f32[3072,1,64]{2,1,0:T(1,128)S(1)} %bitcast.155, f32[]{:T(128)} %broadcast.202), dimensions={1}, to_apply=%bitcast.122.reduce_sub_computation | reduce | bytes 1572868
  304.2 1.9 reshape.240
  306.0 6.1 %all-to-all-start.4 = ((f32[8,1,24576]{2,1,0:T(1,128)}), f32[8,1,24576]{2,1,0:T(1,128)S(1)}, u32[]{:S(2)}, u32[]{:S(2)}) async-start(f32[8,1,24576]{2,1,0:T(1,128)} %reshape.240), calls=%async_computation.4 | async-start | bytes 1572864 | tf_op jit(solution)/shard_map/all_to_all | solution.py:146
  312.2 2.5 reduce.8
  314.7 1.0 reshape.243
  316.5 1.5 fusion.30
  318.0 3.5 copy.79
  321.5 11.2 %all-to-all-done.4 = f32[8,1,24576]{2,1,0:T(1,128)S(1)} async-done(((f32[8,1,24576]{2,1,0:T(1,128)}), f32[8,1,24576]{2,1,0:T(1,128)S(1)}, u32[]{:S(2)}, u32[]{:S(2)}) %all-to-all-start.4) | async-done | bytes 786464 | tf_op jit(solution)/shard_map/all_to_all | solution.py:146
  332.7 0.9 copy-done.6
  333.5 3.9 all-to-all-start.7
  337.5 4.4 reduce.6
  341.9 4.2 reshape.241
  346.2 2.7 copy.73
  348.9 3.3 fusion.37
  352.2 3.6 copy.74
  355.8 52.5 %all-to-all-done.7 = f32[48,64,192]{2,1,0:T(8,128)S(1)} async-done(((f32[48,64,192]{2,1,0:T(8,128)}), f32[48,64,192]{2,1,0:T(8,128)S(1)}, u32[]{:S(2)}, u32[]{:S(2)}) %all-to-all-start.7) | async-done | bytes 2359328 | tf_op jit(solution)/shard_map/all_to_all | solution.py:170
  408.3 4.9 all-to-all-start.5
  413.2 3.5 copy.80
  416.7 4.3 broadcast_in_dim.68
  421.0 96.0 %all-to-all-done.5 = f32[48,64,384]{2,1,0:T(8,128)} async-done(((f32[48,64,384]{2,1,0:T(8,128)}), f32[48,64,384]{2,1,0:T(8,128)}, u32[]{:S(2)}, u32[]{:S(2)}) %all-to-all-start.5) | async-done | bytes 4718624 | tf_op jit(solution)/shard_map/all_to_all | solution.py:169
  517.0 7.2 %copy.75 = f32[6,64,8,384]{3,2,1,0:T(8,128)} copy(f32[6,64,8,384]{3,1,0,2:T(8,128)} %bitcast.39) | data formatting | bytes 9437184 | tf_op jit(solution)/shard_map/all_to_all | solution.py:169
  524.2 5.8 %broadcast_in_dim.66 = f32[1,6,64,3072]{3,2,1,0:T(8,128)} reshape(f32[6,64,8,384]{3,2,1,0:T(8,128)} %copy.75) | data formatting | bytes 9437184 | tf_op jit(solution)/shard_map/broadcast_in_dim | solution.py:172
  (87 shorter events, 7.8 us)
Async XLA Ops:
  7.2 1.3 copy-start.16
  7.2 242.9 %all-gather.3.cloned.1.call-start = ((), (), s32[]{:S(2)}) async-start(), calls=%async_computation.8 | async-start | bytes 10616832 | tf_op jit(solution)/shard_map/all_gather | solution.py:90
  17.0 7.5 %copy-start.7 = (bf16[1,6,64,3072]{3,2,1,0:T(8,128)(2,1)S(1)}, bf16[1,6,64,3072]{3,2,1,0:T(8,128)(2,1)}, u32[]{:S(2)}) copy-start(bf16[1,6,64,3072]{3,2,1,0:T(8,128)(2,1)} %param.16) | copy-start | bytes 7077892
  17.0 67.2 %all-to-all-start = ((bf16[8,2,36864]{2,1,0:T(2,128)(2,1)}), bf16[8,2,36864]{2,1,0:T(2,128)(2,1)S(1)}, u32[]{:S(2)}, u32[]{:S(2)}) async-start(bf16[8,2,36864]{2,1,0:T(2,128)(2,1)} %reshape.236), calls=%async_computation | async-start | bytes 2359296 | tf_op jit(solution)/shard_map/all_to_all | solution.py:99
  45.5 44.7 %copy-start.27 = (s32[48]{0:T(128)S(1)}, s32[48]{0:T(128)}, u32[]{:S(2)}) copy-start(s32[48]{0:T(128)} %param.19) | copy-start | bytes 580
  45.5 44.8 %copy-start.28 = (s32[8]{0:T(128)S(1)}, s32[8]{0:T(128)}, u32[]{:S(2)}) copy-start(s32[8]{0:T(128)} %param.18) | copy-start | bytes 100
  45.5 45.5 %copy-start.10 = (f32[128,3072]{1,0:T(8,128)S(1)}, f32[128,3072]{1,0:T(8,128)}, u32[]{:S(2)}) copy-start(f32[128,3072]{1,0:T(8,128)} %param.12) | copy-start | bytes 4718596
  84.2 1.0 copy-start.3
  85.2 115.8 %all-to-all-start.2 = ((bf16[8,2,73728]{2,1,0:T(2,128)(2,1)}), bf16[8,2,73728]{2,1,0:T(2,128)(2,1)}, u32[]{:S(2)}, u32[]{:S(2)}) async-start(bf16[8,2,73728]{2,1,0:T(2,128)(2,1)} %reshape.238), calls=%async_computation.2 | async-start | bytes 4718592 | tf_op jit(solution)/shard_map/all_to_all | solution.py:98
  90.4 0.5 copy-start.24
  99.3 110.6 %copy-start = (bf16[128,3072]{1,0:T(8,128)(2,1)S(1)}, bf16[128,3072]{1,0:T(8,128)(2,1)}, u32[]{:S(2)}) copy-start(bf16[128,3072]{1,0:T(8,128)(2,1)} %param.11) | copy-start | bytes 2359300
  200.9 30.7 %all-to-all-start.1 = ((bf16[8,64,192]{2,1,0:T(8,128)(2,1)}), bf16[8,64,192]{2,1,0:T(8,128)(2,1)S(1)}, u32[]{:S(2)}, u32[]{:S(2)}) async-start(bf16[8,64,192]{2,1,0:T(8,128)(2,1)} %gather_fusion), calls=%async_computation.1 | async-start | bytes 524288 | tf_op jit(solution)/shard_map/all_to_all | solution.py:103
  210.0 2.8 copy-start.29
  213.6 24.0 %copy-start.22 = (f32[128]{0:T(128)}, f32[128]{0:T(128)S(1)}, u32[]{:S(2)}) copy-start(f32[128]{0:T(128)S(1)} %fusion.20) | copy-start | bytes 1540
  228.5 9.2 %copy-start.1 = (f32[1,128,3072]{2,1,0:T(8,128)S(1)}, f32[1,128,3072]{2,1,0:T(8,128)}, u32[]{:S(2)}) copy-start(f32[1,128,3072]{2,1,0:T(8,128)} %get-tuple-element.7) | copy-start | bytes 4718596
  231.7 6.0 %copy-start.17 = (bf16[8,64,192]{2,1,0:T(8,128)(2,1)}, bf16[8,64,192]{2,1,0:T(8,128)(2,1)S(1)}, u32[]{:S(2)}) copy-start(bf16[8,64,192]{2,1,0:T(8,128)(2,1)S(1)} %all-to-all-done.1) | copy-start | bytes 589828
  231.7 17.1 %all-to-all-start.3 = ((bf16[8,64,384]{2,1,0:T(8,128)(2,1)}), bf16[8,64,384]{2,1,0:T(8,128)(2,1)S(1)}, u32[]{:S(2)}, u32[]{:S(2)}) async-start(bf16[8,64,384]{2,1,0:T(8,128)(2,1)} %gather_fusion.1), calls=%async_computation.3 | async-start | bytes 786432 | tf_op jit(solution)/shard_map/all_to_all | solution.py:102
  237.7 11.9 %copy-start.19 = (f32[1,3072]{1,0:T(1,128)S(1)}, f32[1,3072]{1,0:T(1,128)}, u32[]{:S(2)}) copy-start(f32[1,3072]{1,0:T(1,128)} %param.14) | copy-start | bytes 36868
  237.7 12.4 %copy-start.30 = (f32[128]{0:T(128)}, f32[128]{0:T(128)S(1)}, u32[]{:S(2)}) copy-start(f32[128]{0:T(128)S(1)} %add_rsqrt_fusion.1) | copy-start | bytes 1540
  241.3 17.0 %copy-start.8 = (bf16[64,1536]{1,0:T(8,128)(2,1)}, bf16[64,1536]{1,0:T(8,128)(2,1)S(1)}, u32[]{:S(2)}) copy-start(bf16[64,1536]{1,0:T(8,128)(2,1)S(1)} %reshape.210) | copy-start | bytes 589828
  248.8 0.7 copy-start.11
  250.1 5.4 copy-start.18
  250.1 5.3 copy-start.5
  250.1 8.5 %copy-start.2 = (bf16[1,3072,1536]{2,1,0:T(8,128)(2,1)S(1)}, bf16[1,3072,1536]{2,1,0:T(8,128)(2,1)}, u32[]{:S(2)}) copy-start(bf16[1,3072,1536]{2,1,0:T(8,128)(2,1)} %all-gather.3.cloned.1.call-done) | copy-start | bytes 28311556
  255.4 1.5 copy-start.13
  257.0 4.7 collective-permute-start
  258.6 3.1 copy-start.12
  258.7 3.1 copy-start.20
  261.8 0.9 copy-start.23
  264.7 4.6 copy-start.4
  264.7 4.6 collective-permute-start.1
  271.0 0.7 copy-start.14
  272.9 12.5 %copy-start.9 = (bf16[64,1536]{1,0:T(8,128)(2,1)S(1)}, bf16[64,1536]{1,0:T(8,128)(2,1)}, u32[]{:S(2)}) copy-start(bf16[64,1536]{1,0:T(8,128)(2,1)} %copy-done.8) | copy-start | bytes 589828
  272.9 12.5 %copy-start.21 = (f32[1,3072]{1,0:T(1,128)S(1)}, f32[1,3072]{1,0:T(1,128)}, u32[]{:S(2)}) copy-start(f32[1,3072]{1,0:T(1,128)} %param.14) | copy-start | bytes 36868
  272.9 12.5 %copy-start.26 = (f32[128]{0:T(128)S(1)}, f32[128]{0:T(128)}, u32[]{:S(2)}) copy-start(f32[128]{0:T(128)} %get-tuple-element.11) | copy-start | bytes 1540
  272.9 12.5 %copy-start.31 = (f32[128]{0:T(128)S(1)}, f32[128]{0:T(128)}, u32[]{:S(2)}) copy-start(f32[128]{0:T(128)} %copy-done.30) | copy-start | bytes 1540
  280.0 5.4 %copy-start.15 = (bf16[128,1536]{1,0:T(8,128)(2,1)S(1)}, bf16[128,1536]{1,0:T(8,128)(2,1)}, u32[]{:S(2)}) copy-start(bf16[128,1536]{1,0:T(8,128)(2,1)} %copy-done.14) | copy-start | bytes 1179652
  281.3 24.8 %all-to-all-start.6 = ((f32[8,1,12288]{2,1,0:T(1,128)}), f32[8,1,12288]{2,1,0:T(1,128)}, u32[]{:S(2)}, u32[]{:S(2)}) async-start(f32[8,1,12288]{2,1,0:T(1,128)} %reshape.242), calls=%async_computation.6 | async-start | bytes 786432 | tf_op jit(solution)/shard_map/all_to_all | solution.py:147
  306.0 26.6 %all-to-all-start.4 = ((f32[8,1,24576]{2,1,0:T(1,128)}), f32[8,1,24576]{2,1,0:T(1,128)S(1)}, u32[]{:S(2)}, u32[]{:S(2)}) async-start(f32[8,1,24576]{2,1,0:T(1,128)} %reshape.240), calls=%async_computation.4 | async-start | bytes 1572864 | tf_op jit(solution)/shard_map/all_to_all | solution.py:146
  315.7 0.8 copy-start.25
  332.6 0.9 copy-start.6
  333.5 74.8 %all-to-all-start.7 = ((f32[48,64,192]{2,1,0:T(8,128)}), f32[48,64,192]{2,1,0:T(8,128)S(1)}, u32[]{:S(2)}, u32[]{:S(2)}) async-start(f32[48,64,192]{2,1,0:T(8,128)} %copy.79), calls=%async_computation.7 | async-start | bytes 6291456 | tf_op jit(solution)/shard_map/all_to_all | solution.py:170
  408.3 108.7 %all-to-all-start.5 = ((f32[48,64,384]{2,1,0:T(8,128)}), f32[48,64,384]{2,1,0:T(8,128)}, u32[]{:S(2)}, u32[]{:S(2)}) async-start(f32[48,64,384]{2,1,0:T(8,128)} %copy.74), calls=%async_computation.5 | async-start | bytes 9437184 | tf_op jit(solution)/shard_map/all_to_all | solution.py:169
Sparse Core Ops, SparseCore 0:
  10.2 214.9 all-gather.2
where the time goes:
time: 547 us; the launch traced here: 537 us
  waiting for transfers between devices  307 us (56%)
  local copies, waits for them, and re-layouts  107 us (20%)
  starting transfers between devices  48.9 us (9%)
  other arithmetic  36.5 us (7%)
  matrix products  21.4 us (4%)
  between operations  16.4 us (3%)
    all_to_all x1, waiting for transfers between devices, body(): lax.all_to_all(down_factors[0], 'dp', split_axis=2, concat_axis=0, tiled=...  98.8 us
    all_to_all x1, waiting for transfers between devices, body(): lax.all_to_all(slot_down, 'dp', split_axis=0, concat_axis=2, tiled=True)  96 us
    unnamed x78, local copies, waits for them, and re-layouts  54.6 us
    all_to_all x1, waiting for transfers between devices, body(): lax.all_to_all(slot_up, 'dp', split_axis=0, concat_axis=2, tiled=True)  52.5 us
    all_to_all x1, waiting for transfers between devices, body(): lax.all_to_all(up_factors[0], 'dp', split_axis=2, concat_axis=0, tiled=True)  38.7 us
    unnamed x2, other arithmetic  20.7 us
    all_to_all x1, waiting for transfers between devices, body(): lax.all_to_all(sum_down, 'dp', split_axis=2, concat_axis=0, tiled=True)  11.2 us
  transfers between devices with their start and end apart: 11, of which 7 were waited for; matrix products, arithmetic and copies ran while one was open for 24% of the time, Pallas kernels for 0%

commit v1 on v0

--- a/solution.py
+++ b/solution.py
@@ -4,6 +4,16 @@
 from jax.sharding import PartitionSpec as P
 
 epsilon = 1e-06
+
+
+def process_the_slabs(chunk, along_axis):
+    piece_next = jnp.concatenate(
+        jax.lax.all_to_all(
+            jnp.stack(jnp.split(chunk, jax.lax.axis_size(along_axis), axis=2)), along_axis, 0, 0
+        ),
+        axis=0,
+    )
+    return piece_next
 
 
 def passed_along(value, axis, steps):
@@ -95,7 +105,7 @@
     matches = block_jobs[:, None] == jnp.arange(owners.shape[0], dtype=jnp.int32)[None, :]
     slot_of = jnp.sum(jnp.where(matches, owners[None, :], 0), axis=1)
     spread_down, spread_up = (
-        lax.all_to_all(down_factors[0], "dp", split_axis=2, concat_axis=0, tiled=True),
+        process_the_slabs(down_factors[0], "dp"),
         lax.all_to_all(up_factors[0], "dp", split_axis=2, concat_axis=0, tiled=True),
     )
     down_projection_block, up_block = (

time: 547 us -> 535 us (0.978)
  local copies, waits for them, and re-layouts: 107 us -> 76.9 us
  waiting for transfers between devices: 307 us -> 328 us
    unnamed x78 -> x81, local copies, waits for them, and re-layouts: 54.6 us -> 30.5 us
    all_to_all x1, waiting for transfers between devices: 38.7 us -> 53.7 us  [body(): lax.all_to_all(up_factors[0], 'dp', split_axis=2, concat_axis=0, tiled=True)]
    all_to_all x1 -> x0, local copies, waits for them, and re-layouts: 6.67 us -> none  [body(): lax.all_to_all(down_factors[0], 'dp', split_axis=2, concat_axis=0, tiled=...]
    all_to_all x1, waiting for transfers between devices: 0.01 us -> 5.92 us  [body(): lax.all_to_all(spread_up[slot_of], 'dp', split_axis=0, concat_axis=2, til...]
  transfers between devices with their start and end apart: 11 -> 11, of which waited for: 7 -> 8; matrix products, arithmetic and copies ran while one was open for 24% -> 18% of each run, Pallas kernels for 0% -> 0%
where the time goes in v1:
time: 535 us; the launch traced here: 526 us
  waiting for transfers between devices  328 us (61%)
  local copies, waits for them, and re-layouts  76.9 us (14%)
  starting transfers between devices  46.7 us (9%)
  other arithmetic  36.9 us (7%)
  matrix products  21.5 us (4%)
  between operations  16.2 us (3%)
    all_to_all x1, waiting for transfers between devices, process_the_slabs(): jax.lax.all_to_all(jnp.stack(jnp.split(chunk, jax.lax.axis_size(along_axi...  98.9 us
    all_to_all x1, waiting for transfers between devices, body(): lax.all_to_all(slot_down, 'dp', split_axis=0, concat_axis=2, tiled=True)  96 us
    all_to_all x1, waiting for transfers between devices, body(): lax.all_to_all(up_factors[0], 'dp', split_axis=2, concat_axis=0, tiled=True)  53.7 us
    all_to_all x1, waiting for transfers between devices, body(): lax.all_to_all(slot_up, 'dp', split_axis=0, concat_axis=2, tiled=True)  52.5 us
    unnamed x81, local copies, waits for them, and re-layouts  30.5 us
    unnamed x2, other arithmetic  20.8 us
    all_to_all x1, waiting for transfers between devices, body(): lax.all_to_all(sum_down, 'dp', split_axis=2, concat_axis=0, tiled=True)  11.2 us
  transfers between devices with their start and end apart: 11, of which 8 were waited for; matrix products, arithmetic and copies ran while one was open for 18% of the time, Pallas kernels for 0%

profile of v1, /device:TPU:0, one launch (start us, length us, event | category | flops | bytes accessed | tf_op | source)
XLA Modules:
  0.0 526.2 jit_solution(17402442675074097662)
XLA Ops:
  8.4 3.4 copy.56
  11.9 2.0 bitcast_bitcast_fusion
  13.9 3.1 reshape.240
  17.0 7.5 %all-to-all-start = ((bf16[8,2,36864]{2,1,0:T(2,128)(2,1)}), bf16[8,2,36864]{2,1,0:T(2,128)(2,1)S(1)}, u32[]{:S(2)}, u32[]{:S(2)}) async-start(bf16[8,2,36864]{2,1,0:T(2,128)(2,1)} %reshape.240), calls=%async_computation | async-start | bytes 2359296 | tf_op jit(solution)/shard_map/all_to_all | solution.py:109
  24.5 0.7 fusion.42
  25.3 0.7 fusion.41
  26.7 0.7 fusion.39
  27.5 0.7 fusion.38
  28.2 0.7 fusion.37
  30.4 53.7 %all-to-all-done = bf16[8,2,36864]{2,1,0:T(2,128)(2,1)S(1)} async-done(((bf16[8,2,36864]{2,1,0:T(2,128)(2,1)}), bf16[8,2,36864]{2,1,0:T(2,128)(2,1)S(1)}, u32[]{:S(2)}, u32[]{:S(2)}) %all-to-all-start) | async-done | bytes 1179680 | tf_op jit(solution)/shard_map/all_to_all | solution.py:109
  84.2 1.0 copy-done.3
  85.2 4.4 all-to-all-start.2
  91.0 2.1 select_bitcast_fusion
  93.1 3.6 reshape.241
  96.6 2.7 copy.58
  99.3 2.8 gather_fusion
  102.1 98.9 %all-to-all-done.2 = bf16[8,6,64,384]{3,2,1,0:T(8,128)(2,1)} async-done(((bf16[8,6,64,384]{3,2,1,0:T(8,128)(2,1)}), bf16[8,6,64,384]{3,2,1,0:T(8,128)(2,1)}, u32[]{:S(2)}, u32[]{:S(2)}) %all-to-all-start.2) | async-done | bytes 2359328 | tf_op jit(solution)/shard_map/all_to_all | solution.py:11
  201.0 9.0 %all-to-all-start.1 = ((bf16[8,64,192]{2,1,0:T(8,128)(2,1)}), bf16[8,64,192]{2,1,0:T(8,128)(2,1)S(1)}, u32[]{:S(2)}, u32[]{:S(2)}) async-start(bf16[8,64,192]{2,1,0:T(8,128)(2,1)} %gather_fusion), calls=%async_computation.1 | async-start | bytes 524288 | tf_op jit(solution)/shard_map/all_to_all | solution.py:113
  210.0 1.3 convert_bitcast_fusion
  212.0 0.8 slice.22
  213.7 3.0 gather_fusion.1
  216.7 5.9 %all-to-all-done.1 = bf16[8,64,192]{2,1,0:T(8,128)(2,1)S(1)} async-done(((bf16[8,64,192]{2,1,0:T(8,128)(2,1)}), bf16[8,64,192]{2,1,0:T(8,128)(2,1)S(1)}, u32[]{:S(2)}, u32[]{:S(2)}) %all-to-all-start.1) | async-done | bytes 196640 | tf_op jit(solution)/shard_map/all_to_all | solution.py:113
  222.6 3.5 all-to-all-start.3
  226.8 1.8 copy.59
  228.6 1.2 reshape.213
  229.8 7.6 %all-to-all-done.3 = bf16[8,64,384]{2,1,0:T(8,128)(2,1)S(1)} async-done(((bf16[8,64,384]{2,1,0:T(8,128)(2,1)}), bf16[8,64,384]{2,1,0:T(8,128)(2,1)S(1)}, u32[]{:S(2)}, u32[]{:S(2)}) %all-to-all-start.3) | async-done | bytes 393248 | tf_op jit(solution)/shard_map/all_to_all | solution.py:112
  238.8 5.3 %fusion.2 = f32[128,1536]{1,0:T(8,128)S(1)} fusion(bf16[1,3072,1536]{2,1,0:T(8,128)(2,1)} %all-gather.3.cloned.1.call-done, f32[3072]{0:T(1024)S(1)} %bitcast.200, f32[128]{0:T(128)S(1)} %add_rsqrt_fusion.1, bf16[128,3072]{1,0:T(8,128)(2,1)S(1)} %copy-done, pred[]{:T(512)S(6)} %eq.53), kind=kOutput, calls=%fused_computation.4 | convolution fusion | flops 1209925632 | bytes 11022849 | tf_op jit(solution)/shard_map/dot_general | solution.py:35
  244.1 1.5 fusion.10
  245.7 1.3 collective-permute-start
  247.3 3.1 fusion
  250.5 0.8 fusion.16
  251.9 1.4 fusion.19
  253.3 1.7 collective-permute-start.1
  255.0 1.5 fusion.23
  256.5 1.4 collective-permute-done.1
  258.0 1.7 fusion.34
  261.6 7.2 %reduce.7 = f32[1536,64]{1,0:T(8,128)S(1)} reduce(f32[1536,1,64]{2,1,0:T(1,128)S(1)} %bitcast.179, f32[]{:T(128)} %broadcast.202), dimensions={1}, to_apply=%bitcast.150.reduce_sub_computation | reduce | bytes 786436
  268.8 1.2 reshape.244
  270.1 4.1 all-to-all-start.6
  274.2 1.7 convolution_select_fusion
  275.9 1.8 fusion.6
  277.7 1.7 copy.61
  279.4 13.7 %reduce.5 = f32[3072,64]{1,0:T(8,128)S(1)} reduce(f32[3072,1,64]{2,1,0:T(1,128)S(1)} %bitcast.178, f32[]{:T(128)} %broadcast.202), dimensions={1}, to_apply=%bitcast.148.reduce_sub_computation | reduce | bytes 1572868
  293.0 1.9 reshape.242
  294.9 6.5 %all-to-all-start.4 = ((f32[8,1,24576]{2,1,0:T(1,128)}), f32[8,1,24576]{2,1,0:T(1,128)S(1)}, u32[]{:S(2)}, u32[]{:S(2)}) async-start(f32[8,1,24576]{2,1,0:T(1,128)} %reshape.242), calls=%async_computation.4 | async-start | bytes 1572864 | tf_op jit(solution)/shard_map/all_to_all | solution.py:156
  301.4 2.5 reduce.8
  303.9 1.0 reshape.245
  305.7 1.5 fusion.30
  307.2 3.5 copy.68
  310.7 11.2 %all-to-all-done.4 = f32[8,1,24576]{2,1,0:T(1,128)S(1)} async-done(((f32[8,1,24576]{2,1,0:T(1,128)}), f32[8,1,24576]{2,1,0:T(1,128)S(1)}, u32[]{:S(2)}, u32[]{:S(2)}) %all-to-all-start.4) | async-done | bytes 786464 | tf_op jit(solution)/shard_map/all_to_all | solution.py:156
  321.9 0.9 copy-done.6
  322.8 3.8 all-to-all-start.7
  326.7 4.5 reduce.6
  331.2 4.2 reshape.243
  335.4 2.7 copy.62
  338.1 3.3 fusion.45
  341.4 3.6 copy.63
  345.0 52.5 %all-to-all-done.7 = f32[48,64,192]{2,1,0:T(8,128)S(1)} async-done(((f32[48,64,192]{2,1,0:T(8,128)}), f32[48,64,192]{2,1,0:T(8,128)S(1)}, u32[]{:S(2)}, u32[]{:S(2)}) %all-to-all-start.7) | async-done | bytes 2359328 | tf_op jit(solution)/shard_map/all_to_all | solution.py:180
  397.5 4.8 all-to-all-start.5
  402.3 3.5 copy.69
  405.8 4.3 broadcast_in_dim.68
  410.1 96.0 %all-to-all-done.5 = f32[48,64,384]{2,1,0:T(8,128)} async-done(((f32[48,64,384]{2,1,0:T(8,128)}), f32[48,64,384]{2,1,0:T(8,128)}, u32[]{:S(2)}, u32[]{:S(2)}) %all-to-all-start.5) | async-done | bytes 4718624 | tf_op jit(solution)/shard_map/all_to_all | solution.py:179
  506.1 7.2 %copy.64 = f32[6,64,8,384]{3,2,1,0:T(8,128)} copy(f32[6,64,8,384]{3,1,0,2:T(8,128)} %bitcast.44) | data formatting | bytes 9437184 | tf_op jit(solution)/shard_map/all_to_all | solution.py:179
  513.3 5.8 %broadcast_in_dim.66 = f32[1,6,64,3072]{3,2,1,0:T(8,128)} reshape(f32[6,64,8,384]{3,2,1,0:T(8,128)} %copy.64) | data formatting | bytes 9437184 | tf_op jit(solution)/shard_map/broadcast_in_dim | solution.py:182
  (90 shorter events, 10.8 us)
Async XLA Ops:
  7.2 1.3 copy-start.16
  7.2 231.6 %all-gather.3.cloned.1.call-start = ((), (), s32[]{:S(2)}) async-start(), calls=%async_computation.8 | async-start | bytes 10616832 | tf_op jit(solution)/shard_map/all_gather | solution.py:100
  17.0 7.5 %copy-start.7 = (bf16[1,6,64,3072]{3,2,1,0:T(8,128)(2,1)S(1)}, bf16[1,6,64,3072]{3,2,1,0:T(8,128)(2,1)}, u32[]{:S(2)}) copy-start(bf16[1,6,64,3072]{3,2,1,0:T(8,128)(2,1)} %param.16) | copy-start | bytes 7077892
  17.0 67.2 %all-to-all-start = ((bf16[8,2,36864]{2,1,0:T(2,128)(2,1)}), bf16[8,2,36864]{2,1,0:T(2,128)(2,1)S(1)}, u32[]{:S(2)}, u32[]{:S(2)}) async-start(bf16[8,2,36864]{2,1,0:T(2,128)(2,1)} %reshape.240), calls=%async_computation | async-start | bytes 2359296 | tf_op jit(solution)/shard_map/all_to_all | solution.py:109
  30.4 59.8 %copy-start.27 = (s32[48]{0:T(128)S(1)}, s32[48]{0:T(128)}, u32[]{:S(2)}) copy-start(s32[48]{0:T(128)} %param.19) | copy-start | bytes 580
  30.4 59.8 %copy-start.28 = (s32[8]{0:T(128)S(1)}, s32[8]{0:T(128)}, u32[]{:S(2)}) copy-start(s32[8]{0:T(128)} %param.18) | copy-start | bytes 100
  30.4 60.6 %copy-start.10 = (f32[128,3072]{1,0:T(8,128)S(1)}, f32[128,3072]{1,0:T(8,128)}, u32[]{:S(2)}) copy-start(f32[128,3072]{1,0:T(8,128)} %param.12) | copy-start | bytes 4718596
  84.2 1.0 copy-start.3
  85.2 115.8 %all-to-all-start.2 = ((bf16[8,6,64,384]{3,2,1,0:T(8,128)(2,1)}), bf16[8,6,64,384]{3,2,1,0:T(8,128)(2,1)}, u32[]{:S(2)}, u32[]{:S(2)}) async-start(bf16[8,6,64,384]{3,2,1,0:T(8,128)(2,1)} %fusion.35), calls=%async_computation.2 | async-start | bytes 4718592 | tf_op jit(solution)/shard_map/all_to_all | solution.py:11
  90.4 0.5 copy-start.24
  99.3 110.7 %copy-start = (bf16[128,3072]{1,0:T(8,128)(2,1)S(1)}, bf16[128,3072]{1,0:T(8,128)(2,1)}, u32[]{:S(2)}) copy-start(bf16[128,3072]{1,0:T(8,128)(2,1)} %param.11) | copy-start | bytes 2359300
  201.0 21.6 %all-to-all-start.1 = ((bf16[8,64,192]{2,1,0:T(8,128)(2,1)}), bf16[8,64,192]{2,1,0:T(8,128)(2,1)S(1)}, u32[]{:S(2)}, u32[]{:S(2)}) async-start(bf16[8,64,192]{2,1,0:T(8,128)(2,1)} %gather_fusion), calls=%async_computation.1 | async-start | bytes 524288 | tf_op jit(solution)/shard_map/all_to_all | solution.py:113
  210.0 2.8 copy-start.29
  211.9 14.2 %copy-start.1 = (f32[1,128,3072]{2,1,0:T(8,128)S(1)}, f32[1,128,3072]{2,1,0:T(8,128)}, u32[]{:S(2)}) copy-start(f32[1,128,3072]{2,1,0:T(8,128)} %get-tuple-element.7) | copy-start | bytes 4718596
  213.7 12.4 %copy-start.22 = (f32[128]{0:T(128)}, f32[128]{0:T(128)S(1)}, u32[]{:S(2)}) copy-start(f32[128]{0:T(128)S(1)} %fusion.20) | copy-start | bytes 1540
  222.6 3.5 copy-start.17
  222.6 14.8 %all-to-all-start.3 = ((bf16[8,64,384]{2,1,0:T(8,128)(2,1)}), bf16[8,64,384]{2,1,0:T(8,128)(2,1)S(1)}, u32[]{:S(2)}, u32[]{:S(2)}) async-start(bf16[8,64,384]{2,1,0:T(8,128)(2,1)} %gather_fusion.1), calls=%async_computation.3 | async-start | bytes 786432 | tf_op jit(solution)/shard_map/all_to_all | solution.py:112
  226.0 12.2 %copy-start.19 = (f32[1,3072]{1,0:T(1,128)S(1)}, f32[1,3072]{1,0:T(1,128)}, u32[]{:S(2)}) copy-start(f32[1,3072]{1,0:T(1,128)} %param.14) | copy-start | bytes 36868
  226.1 12.7 %copy-start.30 = (f32[128]{0:T(128)}, f32[128]{0:T(128)S(1)}, u32[]{:S(2)}) copy-start(f32[128]{0:T(128)S(1)} %add_rsqrt_fusion.1) | copy-start | bytes 1540
  229.8 17.2 %copy-start.8 = (bf16[64,1536]{1,0:T(8,128)(2,1)}, bf16[64,1536]{1,0:T(8,128)(2,1)S(1)}, u32[]{:S(2)}) copy-start(bf16[64,1536]{1,0:T(8,128)(2,1)S(1)} %reshape.213) | copy-start | bytes 589828
  237.5 0.7 copy-start.11
  238.7 5.4 %copy-start.18 = (bf16[128,64]{0,1:T(8,128)(2,1)}, bf16[128,64]{0,1:T(8,128)(2,1)S(1)}, u32[]{:S(2)}) copy-start(bf16[128,64]{0,1:T(8,128)(2,1)S(1)} %convolution_convert_fusion.1) | copy-start | bytes 49156
  238.8 5.3 %copy-start.5 = (f32[1,128,3072]{2,1,0:T(8,128)S(1)}, f32[1,128,3072]{2,1,0:T(8,128)}, u32[]{:S(2)}) copy-start(f32[1,128,3072]{2,1,0:T(8,128)} %get-tuple-element.9) | copy-start | bytes 4718596
  238.8 8.5 %copy-start.2 = (bf16[1,3072,1536]{2,1,0:T(8,128)(2,1)S(1)}, bf16[1,3072,1536]{2,1,0:T(8,128)(2,1)}, u32[]{:S(2)}) copy-start(bf16[1,3072,1536]{2,1,0:T(8,128)(2,1)} %all-gather.3.cloned.1.call-done) | copy-start | bytes 28311556
  244.1 1.5 copy-start.13
  245.7 4.7 collective-permute-start
  247.3 3.1 copy-start.12
  247.3 3.1 copy-start.20
  250.4 0.9 copy-start.23
  253.3 4.6 copy-start.4
  253.3 4.6 collective-permute-start.1
  259.7 0.7 copy-start.14
  261.6 12.5 %copy-start.9 = (bf16[64,1536]{1,0:T(8,128)(2,1)S(1)}, bf16[64,1536]{1,0:T(8,128)(2,1)}, u32[]{:S(2)}) copy-start(bf16[64,1536]{1,0:T(8,128)(2,1)} %copy-done.8) | copy-start | bytes 589828
  261.6 12.6 %copy-start.21 = (f32[1,3072]{1,0:T(1,128)S(1)}, f32[1,3072]{1,0:T(1,128)}, u32[]{:S(2)}) copy-start(f32[1,3072]{1,0:T(1,128)} %param.14) | copy-start | bytes 36868
  261.6 12.6 %copy-start.26 = (f32[128]{0:T(128)S(1)}, f32[128]{0:T(128)}, u32[]{:S(2)}) copy-start(f32[128]{0:T(128)} %get-tuple-element.11) | copy-start | bytes 1540
  261.6 12.6 %copy-start.31 = (f32[128]{0:T(128)S(1)}, f32[128]{0:T(128)}, u32[]{:S(2)}) copy-start(f32[128]{0:T(128)} %copy-done.30) | copy-start | bytes 1540
  268.8 5.4 %copy-start.15 = (bf16[128,1536]{1,0:T(8,128)(2,1)S(1)}, bf16[128,1536]{1,0:T(8,128)(2,1)}, u32[]{:S(2)}) copy-start(bf16[128,1536]{1,0:T(8,128)(2,1)} %copy-done.14) | copy-start | bytes 1179652
  270.1 24.8 %all-to-all-start.6 = ((f32[8,1,12288]{2,1,0:T(1,128)}), f32[8,1,12288]{2,1,0:T(1,128)}, u32[]{:S(2)}, u32[]{:S(2)}) async-start(f32[8,1,12288]{2,1,0:T(1,128)} %reshape.244), calls=%async_computation.6 | async-start | bytes 786432 | tf_op jit(solution)/shard_map/all_to_all | solution.py:157
  294.9 27.0 %all-to-all-start.4 = ((f32[8,1,24576]{2,1,0:T(1,128)}), f32[8,1,24576]{2,1,0:T(1,128)S(1)}, u32[]{:S(2)}, u32[]{:S(2)}) async-start(f32[8,1,24576]{2,1,0:T(1,128)} %reshape.242), calls=%async_computation.4 | async-start | bytes 1572864 | tf_op jit(solution)/shard_map/all_to_all | solution.py:156
  304.9 0.8 copy-start.25
  321.9 0.9 copy-start.6
  322.8 74.7 %all-to-all-start.7 = ((f32[48,64,192]{2,1,0:T(8,128)}), f32[48,64,192]{2,1,0:T(8,128)S(1)}, u32[]{:S(2)}, u32[]{:S(2)}) async-start(f32[48,64,192]{2,1,0:T(8,128)} %copy.68), calls=%async_computation.7 | async-start | bytes 6291456 | tf_op jit(solution)/shard_map/all_to_all | solution.py:180
  397.5 108.6 %all-to-all-start.5 = ((f32[48,64,384]{2,1,0:T(8,128)}), f32[48,64,384]{2,1,0:T(8,128)}, u32[]{:S(2)}, u32[]{:S(2)}) async-start(f32[48,64,384]{2,1,0:T(8,128)} %copy.63), calls=%async_computation.5 | async-start | bytes 9437184 | tf_op jit(solution)/shard_map/all_to_all | solution.py:179
Sparse Core Ops, SparseCore 0:
  10.2 214.9 all-gather.2
